TPU v7x, 32 devices: a whole 2x2x4 slice. The times are simulated.
32 devices in a mesh: ord: 8 (over y, x, core), ch: 4 (over z).
Axes of the slice: x: 2, y: 2, z: 4, core: 2. Of those that a mesh axis runs over, the one named last changes fastest.
Arguments:
- field_grid: bfloat16 [2, 64, 2, 352, 1440], P(None, 'ch', None, 'ord'), may hold values from -40 to 40
- norm_gain: float32 [64], P('ch'), may hold values from 0.1 to 1.9
- norm_bias: float32 [64], P('ch'), may hold values from -3 to 3
- order_table: int32 [512], replicated, may hold values from 0 to 511, as said below
- legendre: bfloat16 [512, 2, 352, 360], P(('ord', 'ch')), may hold values from -0.3125 to 0.3125
Outputs:
- coefficients: bfloat16 [512, 2, 2, 2, 64, 360], P(('ord', 'ch'))
Inputs may be any that keep to these rules, and one draw needn't show every extreme that they name: `order_table`: a permutation of the orders in which slots 2 q and 2 q + 1 hold orders p and 511 - p.
All inputs are finite; a program needn't handle non-finite values.
Results may differ from a plain program's by a relative error of at most 0.0062.
Values may be sent and summed in bfloat16 or wider, within the bound.
A program may use at most 128 MiB of HBM per device.

v0:
```python
from functools import partial
import math

import jax
import jax.numpy as jnp
from jax import lax
from jax.sharding import PartitionSpec as P


def slot_table(orders, length):
    sample = jnp.arange(length, dtype=jnp.int32)
    phases = sample[:, None] * orders[None, :] % length
    angles = phases.astype(jnp.float32) * (2.0 * math.pi / length)
    factor = 1.0 / math.sqrt(length)
    stacked = jnp.stack([jnp.cos(angles) * factor, -jnp.sin(angles) * factor], axis=2)
    return stacked.reshape(length, 2 * orders.shape[0]).astype(jnp.bfloat16)


def legendre_sums(arrived, legendre, orders):
    odd_order = orders % 2 == 1
    swapped = jnp.where(
        odd_order[:, None, None, None, None, None], arrived[:, :, :, :, ::-1], arrived
    )
    raw_sums = jnp.einsum(
        "srbcpi,spij->sprbcj", swapped, legendre, preferred_element_type=jnp.float32
    )
    half_degrees = legendre.shape[3]
    degree = (
        2 * jnp.arange(half_degrees, dtype=jnp.int32)[None, :]
        + jnp.arange(2, dtype=jnp.int32)[:, None]
    )
    allowed = degree[None, :, :] >= orders[:, None, None]
    return jnp.where(allowed[:, :, None, None, None, :], raw_sums, 0.0).astype(jnp.bfloat16)


def on_device(field_grid, norm_gain, norm_bias, order_table, legendre):
    batch_size, chan_local, hemis, cycle_local, longitudes = field_grid.shape
    order_total = order_table.shape[0]
    values = field_grid.astype(jnp.float32)
    cell_count = hemis * cycle_local * lax.axis_size("ord") * longitudes
    partial_sum = jnp.sum(values, axis=(2, 3, 4))
    totals, squares = lax.psum((partial_sum, jnp.sum(values * values, axis=(2, 3, 4))), "ord")
    average = totals / cell_count
    spread = squares / cell_count - average * average
    centered = values - average[:, :, None, None, None]
    inverse_scale = lax.rsqrt(spread + 1e-05) * norm_gain[None, :]
    normed = (
        centered * inverse_scale[:, :, None, None, None] + norm_bias[None, :, None, None, None]
    ).astype(jnp.bfloat16)
    twiddle = slot_table(order_table, longitudes)
    flat_rows = normed.reshape(-1, longitudes)
    fourier = lax.dot_general(
        twiddle, flat_rows, (((0,), (1,)), ((), ())), preferred_element_type=jnp.float32
    )
    fourier = fourier.reshape(order_total, 2, batch_size, chan_local, hemis, cycle_local)
    north = fourier[:, :, :, :, 0]
    south = fourier[:, :, :, :, 1]
    halves = jnp.stack([north + south, north - south], axis=4).astype(jnp.bfloat16)
    slot_count = legendre.shape[0]
    channel_groups = lax.axis_size("ch")
    first_slot = (lax.axis_index("ord") * channel_groups + lax.axis_index("ch")) * slot_count
    own_orders = lax.dynamic_slice_in_dim(order_table, first_slot, slot_count)
    transform = partial(legendre_sums, legendre=legendre, orders=own_orders)
    arrived = lax.all_to_all(
        lax.all_to_all(halves, "ord", split_axis=0, concat_axis=5, tiled=True),
        "ch",
        split_axis=0,
        concat_axis=3,
        tiled=True,
    )
    return transform(arrived)


def solution(mesh):
    placed = (
        P(None, "ch", None, "ord", None),
        P("ch"),
        P("ch"),
        P(),
        P(("ord", "ch"), None, None, None),
    )
    return jax.shard_map(
        on_device,
        mesh=mesh,
        in_specs=placed,
        out_specs=P(("ord", "ch"), None, None, None, None, None),
        check_vma=False,
    )
```

profile of v0, /device:TPU:0, one launch (start us, length us, event | category | flops | bytes accessed | tf_op | source)
XLA Modules:
  0.0 532.1 jit_solution(7866468105255323386)
XLA Ops:
  0.0 0.0 copy-start
  0.0 21.6 %convert_reduce_fusion = (f32[2,16]{1,0:T(2,128)S(1)}, f32[2,16]{1,0:T(2,128)S(1)}) fusion(bf16[2,16,2,44,1440]{4,2,3,1,0:T(2,128)(2,1)} %param.5), kind=kLoop, calls=%fused_computation.2 | loop fusion | flops 16220096 | bytes 8110336 | tf_op jit(solution)/shard_map/reduce_sum | solution.py:41
  21.6 0.0 copy-done
  21.6 12.8 %multiply_convert_fusion.1 = (bf16[1440,512,1]{1,0,2:T(8,128)(2,1)S(1)}, bf16[1440,512,1]{1,0,2:T(8,128)(2,1)S(1)}) fusion(s32[512]{0:T(512)S(1)} %copy-done), kind=kLoop, calls=%fused_computation.24 | loop fusion | flops 10321920 | bytes 2951168 | tf_op jit(solution)/shard_map/convert.2
  34.3 1.9 pad_maximum_fusion.1
  36.2 7.4 %copy.27 = bf16[1440,512,2]{0,2,1:T(2,128)(2,1)S(1)} copy(bf16[1440,512,2]{1,0,2:T(8,128)(2,1)} %pad_maximum_fusion.1) | data formatting | bytes 5898240 | tf_op jit(solution)/shard_map/stack | solution.py:15
  43.6 0.0 copy-start.2
  43.6 0.0 copy-start.1
  43.6 3.5 convert_element_type.29
  47.2 6.1 %dot_general.11 = bf16[512,2,1440]{2,1,0:T(2,128)(2,1)S(1)} reshape(bf16[1024,1440]{1,0:T(8,128)(2,1)} %bitcast.26) | data formatting | bytes 5898240 | tf_op jit(solution)/shard_map/dot_general | solution.py:52
  53.3 15.3 %all-reduce = (f32[2,16]{1,0:T(2,128)S(1)}, f32[2,16]{1,0:T(2,128)S(1)}) all-reduce(f32[2,16]{1,0:T(2,128)S(1)} %get-tuple-element.6, f32[2,16]{1,0:T(2,128)S(1)} %get-tuple-element.5), channel_id=1, replica_groups=mesh['ord'=8,'ch'=4] {'ord'}, use_global_device_ids=true, to_apply=%region_3.0 | all-reduce | flops 64 | bytes 512 | tf_op jit(solution)/shard_map/psum | solution.py:42
  68.7 0.0 copy-done.2
  68.7 0.0 copy-done.1
  68.7 14.5 %fusion.2 = bf16[2,16,2,44,1440]{4,2,3,1,0:T(2,128)(2,1)} fusion(bf16[2,16,2,44,1440]{4,2,3,1,0:T(2,128)(2,1)} %param.5, f32[16]{0:T(128)S(1)} %copy-done.1, f32[2,16]{1,0:T(2,128)S(1)} %get-tuple-element.16, f32[2,16]{1,0:T(2,128)S(1)} %get-tuple-element.15), kind=kLoop, calls=%fused_computation.5 | loop fusion | flops 20275200 | bytes 16220480 | tf_op jit(solution)/shard_map/convert_element_type | solution.py:49
  83.2 12.6 %fusion.4 = f32[512,2,2,16,2,44]{0,5,4,3,2,1:T(8,128)S(1)} fusion(bf16[2,16,2,44,1440]{4,2,3,1,0:T(2,128)(2,1)} %fusion.2, bf16[512,2,1440,1,1,1]{2,1,0,5,4,3:T(2,128)(2,1)S(1)} %bitcast.27), kind=kOutput, calls=%fused_computation.9 | convolution fusion | flops 8304721920 | bytes 22593536 | tf_op jit(solution)/shard_map/dot_general | solution.py:52
  95.8 2.3 add_convert_fusion
  98.1 3.3 pad_maximum_fusion
  101.4 40.4 %copy.30 = bf16[512,2,2,16,2,44]{5,4,3,2,1,0:T(2,128)(2,1)} copy(bf16[512,2,2,16,2,44]{0,5,4,3,2,1:T(8,128)(2,1)} %pad_maximum_fusion) | data formatting | bytes 11534336 | tf_op jit(solution)/shard_map/stack | solution.py:58
  141.8 46.0 %reshape.129 = bf16[8,2,180224]{2,1,0:T(2,128)(2,1)} reshape(bf16[512,2,2,16,2,44]{5,4,3,2,1,0:T(2,128)(2,1)} %copy.30) | data formatting | bytes 11534336
  187.9 71.0 %all_to_all.36 = bf16[8,2,180224]{2,1,0:T(2,128)(2,1)} all-to-all(bf16[8,2,180224]{2,1,0:T(2,128)(2,1)} %reshape.129), channel_id=1, replica_groups=mesh['ord'=8,'ch'=4] {'ord'}, dimensions={0} | all-to-all | bytes 11534336 | tf_op jit(solution)/shard_map/all_to_all | solution.py:65
  258.8 50.2 %reshape.130 = bf16[512,2,2,16,2,44]{5,4,3,2,1,0:T(2,128)(2,1)} reshape(bf16[8,2,180224]{2,1,0:T(2,128)(2,1)} %all_to_all.36) | data formatting | bytes 11534336
  309.0 44.8 %copy.41 = bf16[8,64,2,2,16,2,44]{1,4,6,0,5,3,2:T(8,128)(2,1)} copy(bf16[8,64,2,2,16,2,44]{6,5,4,3,2,1,0:T(2,128)(2,1)} %bitcast.23) | data formatting | bytes 11534336 | tf_op jit(solution)/shard_map/all_to_all | solution.py:65
  353.8 18.0 %copy.33 = bf16[64,2,2,16,2,352]{5,3,4,2,1,0:T(8,128)(2,1)} copy(bf16[64,2,2,16,2,352]{0,3,5,4,2,1:T(8,128)(2,1)} %bitcast.24) | data formatting | bytes 11534336 | tf_op jit(solution)/shard_map/all_to_all | solution.py:65
  371.8 5.5 %all-to-all-start.1 = ((bf16[64,2,2,16,2,352]{5,3,4,2,1,0:T(8,128)(2,1)}), bf16[64,2,2,16,2,352]{5,3,4,2,1,0:T(8,128)(2,1)}, u32[]{:S(2)}, u32[]{:S(2)}) async-start(bf16[64,2,2,16,2,352]{5,3,4,2,1,0:T(8,128)(2,1)} %copy.33), calls=%async_computation.1 | async-start | bytes 12582912 | tf_op jit(solution)/shard_map/all_to_all | solution.py:64
  377.4 0.1 fusion.20
  377.5 0.1 broadcast_compare_fusion
  377.6 137.6 %all-to-all-done.1 = bf16[64,2,2,16,2,352]{5,3,4,2,1,0:T(8,128)(2,1)} async-done(((bf16[64,2,2,16,2,352]{5,3,4,2,1,0:T(8,128)(2,1)}), bf16[64,2,2,16,2,352]{5,3,4,2,1,0:T(8,128)(2,1)}, u32[]{:S(2)}, u32[]{:S(2)}) %all-to-all-start.1) | async-done | bytes 5767200 | tf_op jit(solution)/shard_map/all_to_all | solution.py:64
  515.2 4.0 copy.34
  519.1 3.3 reverse_select_fusion
  522.4 9.7 %select_convert_fusion = bf16[16,2,2,2,64,360]{5,4,3,2,1,0:T(8,128)(2,1)} fusion(pred[16,2,360]{2,1,0:T(4,128)(4,1)S(1)} %broadcast_compare_fusion, bf16[16,2,352,360]{3,2,1,0:T(8,128)(2,1)} %param.9, bf16[16,2,2,64,2,352]{5,3,4,2,1,0:T(8,128)(2,1)S(1)} %reverse_select_fusion), kind=kOutput, calls=%fused_computation.7 | convolution fusion | flops 2082078720 | bytes 19787008 | tf_op jit(solution)/shard_map/srbcpi,spij->sprbcj/dot_general | solution.py:24
  (3 shorter events, 0.0 us)
Async XLA Ops:
  0.0 21.6 %copy-start = (s32[512]{0:T(512)S(1)}, s32[512]{0:T(512)}, u32[]{:S(2)}) copy-start(s32[512]{0:T(512)} %param.8) | copy-start | bytes 6148
  43.6 25.0 %copy-start.2 = (f32[16]{0:T(128)S(1)}, f32[16]{0:T(128)}, u32[]{:S(2)}) copy-start(f32[16]{0:T(128)} %param.6) | copy-start | bytes 196
  43.6 25.0 %copy-start.1 = (f32[16]{0:T(128)S(1)}, f32[16]{0:T(128)}, u32[]{:S(2)}) copy-start(f32[16]{0:T(128)} %param.7) | copy-start | bytes 196
  371.8 143.3 %all-to-all-start.1 = ((bf16[64,2,2,16,2,352]{5,3,4,2,1,0:T(8,128)(2,1)}), bf16[64,2,2,16,2,352]{5,3,4,2,1,0:T(8,128)(2,1)}, u32[]{:S(2)}, u32[]{:S(2)}) async-start(bf16[64,2,2,16,2,352]{5,3,4,2,1,0:T(8,128)(2,1)} %copy.33), calls=%async_computation.1 | async-start | bytes 12582912 | tf_op jit(solution)/shard_map/all_to_all | solution.py:64
where the time goes:
time: 536 us; the launch traced here: 532 us
  local copies, waits for them, and re-layouts  220 us (41%)
  waiting for transfers between devices  138 us (26%)
  blocking collectives  86.3 us (16%)
  other arithmetic  59.8 us (11%)
  matrix products  22.3 us (4%)
  starting transfers between devices  5.52 us (1%)
    all_to_all x1, waiting for transfers between devices, on_device(): lax.all_to_all(lax.all_to_all(halves, 'ord', split_axis=0, concat_axis=5,...  138 us
    unnamed x8, local copies, waits for them, and re-layouts  96.2 us
    all_to_all x1, blocking collectives, on_device(): lax.all_to_all(halves, 'ord', split_axis=0, concat_axis=5, tiled=True)  71 us
    all_to_all x2, local copies, waits for them, and re-layouts, on_device(): lax.all_to_all(halves, 'ord', split_axis=0, concat_axis=5, tiled=True)  62.8 us
    another operation x1, local copies, waits for them, and re-layouts, on_device(): jnp.stack([north + south, north - south], axis=4).astype(jnp.bfloat16)  40.4 us
    reduce_sum x1, other arithmetic, on_device(): partial_sum = jnp.sum(values, axis=(2, 3, 4))  21.6 us
    psum x1, blocking collectives, on_device(): lax.psum((partial_sum, jnp.sum(values * values, axis=(2, 3, 4))), 'ord')  15.3 us
    another operation x2, other arithmetic  15 us
  transfers between devices with their start and end apart: 1, of which 1 were waited for; matrix products, arithmetic and copies ran while one was open for 0% of the time, Pallas kernels for 0%

commit v1 on v0

--- a/solution.py
+++ b/solution.py
@@ -4,7 +4,14 @@
 import jax
 import jax.numpy as jnp
 from jax import lax
+from jax.experimental import pallas as pl
+from jax.experimental.pallas import tpu as pltpu
 from jax.sharding import PartitionSpec as P
+
+MESH = pl.DeviceIdType.MESH
+LANES = 128
+GROUP = 128
+QUAD = 4
 
 
 def slot_table(orders, length):
@@ -33,7 +40,7 @@
     return jnp.where(allowed[:, :, None, None, None, :], raw_sums, 0.0).astype(jnp.bfloat16)
 
 
-def on_device(field_grid, norm_gain, norm_bias, order_table, legendre):
+def general_path(field_grid, norm_gain, norm_bias, order_table, legendre):
     batch_size, chan_local, hemis, cycle_local, longitudes = field_grid.shape
     order_total = order_table.shape[0]
     values = field_grid.astype(jnp.float32)
@@ -71,6 +78,321 @@
     return transform(arrived)
 
 
+def angle_tables(orders, length):
+    factor = 1.0 / math.sqrt(length)
+    step = 2.0 * math.pi / length
+    fine = orders[:, None] * jnp.arange(LANES, dtype=jnp.int32)[None, :] % length
+    coarse = orders[:, None] * (LANES * jnp.arange(LANES, dtype=jnp.int32))[None, :] % length
+    fine = fine.astype(jnp.float32) * step
+    coarse = coarse.astype(jnp.float32) * step
+    return jnp.stack([jnp.cos(fine) * factor, jnp.sin(fine) * factor, jnp.cos(coarse), jnp.sin(coarse)])
+
+
+def exchange_kernel(
+    sizes, field, tables, signs, gain, bias, out,
+    grid, rows, packed, twiddle, sending, stats, stats_in, norms,
+    field_sem, stats_out_sem, stats_in_sem, send_sem, recv_sem, own_sem,
+):
+    n_ord, n_ch, cell_count = sizes
+    total = n_ord * n_ch
+    fields, hemis, cycles, length = grid.shape
+    groups = twiddle.shape[0]
+    steps = sending.shape[1]
+    tiles = rows.shape[1]
+    own_ord, own_ch = lax.axis_index("ord"), lax.axis_index("ch")
+    me = own_ord * n_ch + own_ch
+    parts = field_sem.shape[0]
+    per_part = fields // parts
+
+    def load(part):
+        span = pl.ds(part * per_part, per_part)
+        return pltpu.make_async_copy(field.at[span], grid.at[span], field_sem.at[part])
+
+    for part in range(parts):
+        load(part).start()
+
+    barrier = pltpu.get_barrier_semaphore()
+
+    def greet(hop, carry):
+        peer = lax.rem(me + hop, total)
+        pl.semaphore_signal(
+            barrier, inc=1, device_id=(peer // n_ch, lax.rem(peer, n_ch)), device_id_type=MESH
+        )
+        return carry
+
+    lax.fori_loop(1, total, greet, 0)
+
+    def fold(values):
+        summed = values[:, :LANES]
+        for tile in range(1, tiles - 1):
+            summed += values[:, tile * LANES : (tile + 1) * LANES]
+        rest = values[:, (tiles - 1) * LANES :]
+        blank = jnp.zeros((1, LANES - rest.shape[1]), jnp.float32)
+        return summed + jnp.concatenate([rest, blank], axis=1)
+
+    for part in range(parts):
+        load(part).wait()
+
+        def measure(at, carry, part=part):
+            row = part * per_part + at
+            first = grid[row, 0].astype(jnp.float32)
+            second = grid[row, 1].astype(jnp.float32)
+            stats[pl.ds(row, 1), :] = fold(jnp.sum(first + second, axis=0, keepdims=True))
+            stats[pl.ds(fields + row, 1), :] = fold(
+                jnp.sum(first * first + second * second, axis=0, keepdims=True)
+            )
+            return carry
+
+        lax.fori_loop(0, per_part, measure, 0)
+
+    pl.semaphore_wait(barrier, total - 1)
+
+    def stats_copy(hop):
+        peer = lax.rem(own_ord + hop, n_ord)
+        return pltpu.make_async_remote_copy(
+            src_ref=stats,
+            dst_ref=stats_in.at[own_ord],
+            send_sem=stats_out_sem.at[hop],
+            recv_sem=stats_in_sem.at[own_ord],
+            device_id=(peer, own_ch),
+            device_id_type=MESH,
+        )
+
+    for hop in range(1, n_ord):
+        stats_copy(hop).start()
+    stats_in[own_ord] = stats[...]
+
+    def build(group, carry):
+        span = pl.ds(pl.multiple_of(group * GROUP, GROUP), GROUP)
+        cos_fine, sin_fine = tables[0, span, :], tables[1, span, :]
+        cos_coarse, sin_coarse = tables[2, span, :], tables[3, span, :]
+        for tile in range(tiles):
+            columns = slice(tile * LANES, (tile + 1) * LANES)
+            cos_at, sin_at = cos_coarse[:, tile : tile + 1], sin_coarse[:, tile : tile + 1]
+            twiddle[group, :GROUP, columns] = (cos_at * cos_fine - sin_at * sin_fine).astype(jnp.bfloat16)
+            twiddle[group, GROUP:, columns] = (-(sin_at * cos_fine + cos_at * sin_fine)).astype(jnp.bfloat16)
+        return carry
+
+    lax.fori_loop(0, groups, build, 0)
+
+    for hop in range(1, n_ord):
+        peer = lax.rem(own_ord + hop, n_ord)
+        pltpu.make_async_remote_copy(
+            src_ref=stats, dst_ref=stats_in.at[peer], send_sem=stats_out_sem.at[hop],
+            recv_sem=stats_in_sem.at[peer], device_id=(peer, own_ch), device_id_type=MESH,
+        ).wait()
+
+    merged = stats_in[0]
+    for source in range(1, n_ord):
+        merged = merged + stats_in[source]
+    merged = jnp.sum(merged, axis=1, keepdims=True)
+    average = merged[:fields] / cell_count
+    spread = merged[fields:] / cell_count - average * average
+    scale = lax.rsqrt(spread + 1e-05) * gain[:, :1]
+    norms[0] = jnp.broadcast_to(average, (fields, LANES))
+    norms[1] = jnp.broadcast_to(scale, (fields, LANES))
+    norms[2] = bias[...]
+
+    def normalize(at, carry):
+        shift = norms[0, pl.ds(at, 1), :]
+        factor = norms[1, pl.ds(at, 1), :]
+        offset = norms[2, pl.ds(at, 1), :]
+        for hemi in range(hemis):
+            for tile in range(tiles):
+                piece = grid[at, hemi, :, tile * LANES : min((tile + 1) * LANES, length)]
+                wide = piece.shape[1]
+                piece = (piece.astype(jnp.float32) - shift[:, :wide]) * factor[:, :wide] + offset[:, :wide]
+                if wide < LANES:
+                    piece = jnp.concatenate(
+                        [piece, jnp.zeros((cycles, LANES - wide), jnp.float32)], axis=1
+                    )
+                rows[hemi, tile, pl.ds(at, cycles, stride=fields), :] = piece
+        return carry
+
+    lax.fori_loop(0, fields, normalize, 0)
+
+    lane = lax.broadcasted_iota(jnp.int32, (GROUP, LANES), 1)
+    low = lane // fields % 2 == 0
+    high = lane // (2 * fields) % 2 == 0
+
+    def swap(mask, upper, lower, amount):
+        return (
+            jnp.where(mask, upper, pltpu.roll(lower, amount, 1)),
+            jnp.where(mask, pltpu.roll(upper, LANES - amount, 1), lower),
+        )
+
+    def advance(step, carry):
+        span = pl.ds(pl.multiple_of(step * LANES, LANES), LANES)
+        for hemi in range(hemis):
+            for tile in range(tiles):
+                packed[hemi * LANES : (hemi + 1) * LANES, tile * LANES : (tile + 1) * LANES] = rows[
+                    hemi, tile, span, :
+                ].astype(jnp.bfloat16)
+
+        def transform(group, inner):
+            spectrum = lax.dot_general(
+                twiddle[group], packed[...], (((1,), (1,)), ((), ())),
+                preferred_element_type=jnp.float32,
+            )
+            north, south = spectrum[:, :LANES], spectrum[:, LANES:] * signs[group]
+            even, odd = north + south, north - south
+            a, b, c, d = even[:GROUP], even[GROUP:], odd[:GROUP], odd[GROUP:]
+            a, b = swap(low, a, b, fields)
+            c, d = swap(low, c, d, fields)
+            a, c = swap(high, a, c, 2 * fields)
+            b, d = swap(high, b, d, 2 * fields)
+            each = GROUP // sending.shape[3]
+            for at, piece in enumerate((a, b, c, d)):
+                sending[pl.ds(group * each, each), step, at] = piece.astype(jnp.bfloat16).reshape(
+                    each, GROUP // each, LANES
+                )
+            return inner
+
+        lax.fori_loop(0, groups, transform, 0)
+
+        def send(hop, inner):
+            peer = lax.rem(me + hop, total)
+            pltpu.make_async_remote_copy(
+                src_ref=sending.at[peer, step],
+                dst_ref=out.at[own_ch, own_ord, step],
+                send_sem=send_sem.at[peer],
+                recv_sem=recv_sem.at[me],
+                device_id=(peer // n_ch, lax.rem(peer, n_ch)),
+                device_id_type=MESH,
+            ).start()
+            return inner
+
+        lax.fori_loop(1, total, send, 0)
+        return carry
+
+    lax.fori_loop(0, steps, advance, 0)
+    own = pltpu.make_async_copy(sending.at[me], out.at[own_ch, own_ord], own_sem)
+    own.start()
+
+    def finish(hop, carry):
+        peer = lax.rem(me + hop, total)
+        pltpu.make_async_remote_copy(
+            src_ref=sending.at[peer],
+            dst_ref=out.at[lax.rem(peer, n_ch), peer // n_ch],
+            send_sem=send_sem.at[peer],
+            recv_sem=recv_sem.at[peer],
+            device_id=(peer // n_ch, lax.rem(peer, n_ch)),
+            device_id_type=MESH,
+        ).wait()
+        return carry
+
+    lax.fori_loop(1, total, finish, 0)
+    own.wait()
+
+
+def legendre_kernel(orders, arrived, legendre, out, wide):
+    slot = pl.program_id(0)
+    sources, depth, lanes = wide.shape
+    slots = orders.shape[0]
+    cycles = depth // slots
+
+    @pl.when(slot == 0)
+    def _():
+        for source in range(sources):
+            wide[source] = arrived[source].astype(jnp.float32)
+
+    half = lanes // 2
+    turned = [
+        wide[source, pl.ds(slot, cycles, stride=slots), :].T.astype(jnp.bfloat16)
+        for source in range(sources)
+    ]
+    batch, local = out.shape[3], out.shape[4] // sources
+    order = orders[slot]
+    for parity in range(2):
+        left = jnp.concatenate([t[parity * half : (parity + 1) * half] for t in turned], axis=0)
+        sums = jnp.dot(left, legendre[0, parity], preferred_element_type=jnp.float32)
+        degree = 2 * lax.broadcasted_iota(jnp.int32, sums.shape, 1) + parity
+        sums = jnp.where(degree >= order, sums, 0.0).astype(jnp.bfloat16)
+        for source in range(sources):
+            out[0, parity, :, :, source * local : (source + 1) * local, :] = sums[
+                source * half : (source + 1) * half
+            ].reshape(2, batch, local, sums.shape[1])
+
+
+def kernel_path(field_grid, norm_gain, norm_bias, order_table, legendre):
+    batch, local, hemis, cycles, length = field_grid.shape
+    n_ord, n_ch = lax.axis_size("ord"), lax.axis_size("ch")
+    order_total, slots = order_table.shape[0], legendre.shape[0]
+    fields = batch * local
+    groups = order_total // GROUP
+    tiles = -(-length // LANES)
+    steps = cycles // QUAD
+    total = n_ord * n_ch
+    tables = angle_tables(order_table, length)
+    sign = (1 - 2 * (order_table % 2)).astype(jnp.float32).reshape(groups, 1, GROUP, 1)
+    signs = jnp.broadcast_to(sign, (groups, 2, GROUP, LANES)).reshape(groups, 2 * GROUP, LANES)
+    gain = jnp.broadcast_to(norm_gain[None, :, None], (batch, local, LANES)).reshape(fields, LANES)
+    bias = jnp.broadcast_to(norm_bias[None, :, None], (batch, local, LANES)).reshape(fields, LANES)
+    vmem = pl.BlockSpec(memory_space=pltpu.VMEM)
+    hbm = pl.BlockSpec(memory_space=pltpu.HBM)
+    padded = -(-cycles // 8) * 8 * fields
+    arrived = pl.pallas_call(
+        partial(exchange_kernel, (n_ord, n_ch, hemis * cycles * n_ord * length)),
+        out_shape=jax.ShapeDtypeStruct((n_ch, n_ord, steps, QUAD, slots, LANES), jnp.bfloat16),
+        in_specs=[hbm, vmem, vmem, vmem, vmem],
+        out_specs=hbm,
+        scratch_shapes=[
+            pltpu.VMEM((fields, hemis, cycles, length), jnp.bfloat16),
+            pltpu.VMEM((hemis, tiles, padded, LANES), jnp.float32),
+            pltpu.VMEM((hemis * LANES, tiles * LANES), jnp.bfloat16),
+            pltpu.VMEM((groups, 2 * GROUP, tiles * LANES), jnp.bfloat16),
+            pltpu.VMEM((total, steps, QUAD, slots, LANES), jnp.bfloat16),
+            pltpu.VMEM((2 * fields, LANES), jnp.float32),
+            pltpu.VMEM((n_ord, 2 * fields, LANES), jnp.float32),
+            pltpu.VMEM((3, fields, LANES), jnp.float32),
+            pltpu.SemaphoreType.DMA((8,)),
+            pltpu.SemaphoreType.DMA((n_ord,)),
+            pltpu.SemaphoreType.DMA((n_ord,)),
+            pltpu.SemaphoreType.DMA((total,)),
+            pltpu.SemaphoreType.DMA((total,)),
+            pltpu.SemaphoreType.DMA,
+        ],
+        compiler_params=pltpu.CompilerParams(
+            collective_id=0, has_side_effects=True, vmem_limit_bytes=60 * 2**20
+        ),
+        name="spectral_exchange",
+    )(field_grid.reshape(fields, hemis, cycles, length), tables, signs, gain, bias)
+    depth = n_ord * cycles
+    arrived = arrived.reshape(n_ch, depth * slots, LANES)
+    own = lax.axis_index("ord") * n_ch + lax.axis_index("ch")
+    own_orders = lax.dynamic_slice_in_dim(order_table, own * slots, slots)
+    half_degrees = legendre.shape[3]
+    return pl.pallas_call(
+        legendre_kernel,
+        grid=(slots,),
+        out_shape=jax.ShapeDtypeStruct((slots, 2, 2, batch, n_ch * local, half_degrees), jnp.bfloat16),
+        in_specs=[
+            pl.BlockSpec(memory_space=pltpu.SMEM),
+            pl.BlockSpec((n_ch, depth * slots, LANES), lambda s: (0, 0, 0)),
+            pl.BlockSpec((1, 2, depth, half_degrees), lambda s: (s, 0, 0, 0)),
+        ],
+        out_specs=pl.BlockSpec(
+            (1, 2, 2, batch, n_ch * local, half_degrees), lambda s: (s, 0, 0, 0, 0, 0)
+        ),
+        scratch_shapes=[pltpu.VMEM((n_ch, depth * slots, LANES), jnp.float32)],
+        compiler_params=pltpu.CompilerParams(vmem_limit_bytes=60 * 2**20),
+        name="legendre_sums",
+    )(own_orders, arrived, legendre)
+
+
+def on_device(field_grid, norm_gain, norm_bias, order_table, legendre):
+    batch, local, hemis, cycles, _ = field_grid.shape
+    fits = (
+        batch * local * QUAD == LANES
+        and hemis == 2
+        and cycles % QUAD == 0
+        and legendre.shape[0] == 16
+        and order_table.shape[0] % GROUP == 0
+    )
+    path = kernel_path if fits else general_path
+    return path(field_grid, norm_gain, norm_bias, order_table, legendre)
+
+
 def solution(mesh):
     placed = (
         P(None, "ch", None, "ord", None),

time: 536 us -> 200 us (0.37)
  local copies, waits for them, and re-layouts: 220 us -> 12.5 us
  Pallas kernels: 0 us -> 183 us
  waiting for transfers between devices: 138 us -> 0 us
  blocking collectives: 86.3 us -> 0 us
  other arithmetic: 59.8 us -> 3.98 us
  matrix products: 22.3 us -> 0 us
  starting transfers between devices: 5.52 us -> 0 us
    pallas_call x0 -> x2, Pallas kernels: none -> 183 us  [the longest x1 163 us: kernel_path(): pl.pallas_call(partial(exchange_kernel, (n_ord, n_ch, hemis * cycles * n_...]
    all_to_all x1 -> x0, waiting for transfers between devices: 138 us -> none  [on_device(): lax.all_to_all(lax.all_to_all(halves, 'ord', split_axis=0, concat_axis=5,...]
    unnamed x8 -> x9, local copies, waits for them, and re-layouts: 96.2 us -> 9.31 us
    all_to_all x1 -> x0, blocking collectives: 71 us -> none  [on_device(): lax.all_to_all(halves, 'ord', split_axis=0, concat_axis=5, tiled=True)]
    all_to_all x3 -> x0, local copies, waits for them, and re-layouts: 66.8 us -> none  [the longest x2 62.8 us: on_device(): lax.all_to_all(halves, 'ord', split_axis=0, concat_axis=5, tiled=True)]
    another operation x2 -> x0, local copies, waits for them, and re-layouts: 47.8 us -> none  [the longest x1 40.4 us: on_device(): jnp.stack([north + south, north - south], axis=4).astype(jnp.bfloat16)]
    dot_general x2 -> x0, matrix products: 22.3 us -> none  [the longest x1 12.6 us: on_device(): lax.dot_general(twiddle, flat_rows, (((0,), (1,)), ((), ())), preferred_e...]
    reduce_sum x1 -> x0, other arithmetic: 21.6 us -> none  [on_device(): partial_sum = jnp.sum(values, axis=(2, 3, 4))]
  transfers between devices with their start and end apart: 1 -> 0, of which waited for: 1 -> 0; matrix products, arithmetic and copies ran while one was open for 0% -> 0% of each run, Pallas kernels for 0% -> 0%
where the time goes in v1:
time: 200 us
  Pallas kernels  183 us (92%)
  local copies, waits for them, and re-layouts  12.5 us (6%)
  other arithmetic  3.98 us (2%)
    pallas_call x1, Pallas kernels, kernel_path(): pl.pallas_call(partial(exchange_kernel, (n_ord, n_ch, hemis * cycles * n_...  163 us
    pallas_call x1, Pallas kernels, kernel_path(): pl.pallas_call(legendre_kernel, grid=(slots,), out_shape=jax.ShapeDtypeSt...  20.1 us
    unnamed x9, local copies, waits for them, and re-layouts  9.31 us

profile of v1, /device:TPU:0, one launch (start us, length us, event | category | flops | bytes accessed | tf_op | source)
XLA Modules:
  0.0 199.6 jit_solution(16857159897472542892)
XLA Ops:
  0.0 2.9 %fusion.7 = (f32[1,512,128]{2,1,0:T(8,128)S(1)}, f32[1,512,128]{2,1,0:T(8,128)S(1)}, f32[1,512,128]{2,1,0:T(8,128)S(1)}, f32[1,512,128]{2,1,0:T(8,128)S(1)}) fusion(s32[128]{0:T(128)S(1)} %iota_multiply_fusion, s32[512]{0:T(512)} %param.8), kind=kLoop, calls=%fused_computation.11 | loop fusion | flops 1310720 | bytes 1051136 | tf_op jit(solution)/shard_map/cos | solution.py:88
  2.9 1.0 pad_maximum_fusion.tables
  4.0 0.0 copy-start
  4.0 0.0 copy-start.1
  4.0 0.0 copy-start.2
  4.0 9.3 %copy.6 = bf16[2,16,2,44,1440]{4,3,2,1,0:T(8,128)(2,1)} copy(bf16[2,16,2,44,1440]{4,2,3,1,0:T(2,128)(2,1)} %param.5) | data formatting | bytes 16220160 | tf_op args[0]
  13.3 0.0 copy-done
  13.3 1.0 broadcast_in_dim.38.signs
  14.3 0.0 copy-done.1
  14.3 0.1 broadcast_in_dim.40
  14.4 0.7 broadcast_in_dim.41.gain
  15.1 0.0 copy-done.2
  15.1 0.1 broadcast_in_dim.43
  15.2 0.7 broadcast_in_dim.44.bias
  15.8 163.1 %spectral_exchange.1 = bf16[4,8,11,4,16,128]{5,4,3,2,1,0:T(8,128)(2,1)} custom-call(bf16[32,2,44,1440]{3,2,1,0:T(8,128)(2,1)} %bitcast.9, f32[4,512,128]{2,1,0:T(8,128)} %pad_maximum_fusion.tables, f32[4,256,128]{2,1,0:T(8,128)} %broadcast_in_dim.38.signs, f32[32,128]{1,0:T(8,128)} %broadcast_in_dim.41.gain, f32[32,128]{1,0:T(8,128)} %broadcast_in_dim.44.bias), custom_call_target="tpu_custom_call" | custom-call | tf_op jit(solution)/shard_map/spectral_exchange/pallas_call | solution.py:334
  178.9 0.6 dynamic_slice.3.orders
  179.5 20.1 %legendre_sums.1 = bf16[16,2,2,2,64,360]{5,4,3,2,1,0:T(8,128)(2,1)} custom-call(s32[16]{0:T(128)} %dynamic_slice.3.orders, bf16[4,5632,128]{2,1,0:T(8,128)(2,1)} %bitcast.10, bf16[16,2,352,360]{3,2,1,0:T(8,128)(2,1)} %legendre.1), custom_call_target="tpu_custom_call" | custom-call | tf_op jit(solution)/shard_map/legendre_sums/pallas_call | solution.py:365
  (6 shorter events, 0.0 us)
Async XLA Ops:
  4.0 9.3 %copy-start = (s32[512]{0:T(512)S(1)}, s32[512]{0:T(512)}, u32[]{:S(2)}) copy-start(s32[512]{0:T(512)} %param.8) | copy-start | bytes 6148
  4.0 10.4 %copy-start.1 = (f32[16]{0:T(128)S(1)}, f32[16]{0:T(128)}, u32[]{:S(2)}) copy-start(f32[16]{0:T(128)} %param.6) | copy-start | bytes 196
  4.0 11.1 %copy-start.2 = (f32[16]{0:T(128)S(1)}, f32[16]{0:T(128)}, u32[]{:S(2)}) copy-start(f32[16]{0:T(128)} %param.7) | copy-start | bytes 196

commit v2 on v1

v2 whole, which is shorter than its diff:
```python
from functools import partial
import math

import jax
import jax.numpy as jnp
from jax import lax
from jax.experimental import pallas as pl
from jax.experimental.pallas import tpu as pltpu
from jax.sharding import PartitionSpec as P

MESH = pl.DeviceIdType.MESH
LANES = 128
GROUP = 128
QUAD = 4
PITCH = 40


def slot_table(orders, length):
    sample = jnp.arange(length, dtype=jnp.int32)
    phases = sample[:, None] * orders[None, :] % length
    angles = phases.astype(jnp.float32) * (2.0 * math.pi / length)
    factor = 1.0 / math.sqrt(length)
    stacked = jnp.stack([jnp.cos(angles) * factor, -jnp.sin(angles) * factor], axis=2)
    return stacked.reshape(length, 2 * orders.shape[0]).astype(jnp.bfloat16)


def legendre_sums(arrived, legendre, orders):
    odd_order = orders % 2 == 1
    swapped = jnp.where(
        odd_order[:, None, None, None, None, None], arrived[:, :, :, :, ::-1], arrived
    )
    raw_sums = jnp.einsum(
        "srbcpi,spij->sprbcj", swapped, legendre, preferred_element_type=jnp.float32
    )
    half_degrees = legendre.shape[3]
    degree = (
        2 * jnp.arange(half_degrees, dtype=jnp.int32)[None, :]
        + jnp.arange(2, dtype=jnp.int32)[:, None]
    )
    allowed = degree[None, :, :] >= orders[:, None, None]
    return jnp.where(allowed[:, :, None, None, None, :], raw_sums, 0.0).astype(jnp.bfloat16)


def general_path(field_grid, norm_gain, norm_bias, order_table, legendre):
    batch_size, chan_local, hemis, cycle_local, longitudes = field_grid.shape
    order_total = order_table.shape[0]
    values = field_grid.astype(jnp.float32)
    cell_count = hemis * cycle_local * lax.axis_size("ord") * longitudes
    partial_sum = jnp.sum(values, axis=(2, 3, 4))
    totals, squares = lax.psum((partial_sum, jnp.sum(values * values, axis=(2, 3, 4))), "ord")
    average = totals / cell_count
    spread = squares / cell_count - average * average
    centered = values - average[:, :, None, None, None]
    inverse_scale = lax.rsqrt(spread + 1e-05) * norm_gain[None, :]
    normed = (
        centered * inverse_scale[:, :, None, None, None] + norm_bias[None, :, None, None, None]
    ).astype(jnp.bfloat16)
    twiddle = slot_table(order_table, longitudes)
    flat_rows = normed.reshape(-1, longitudes)
    fourier = lax.dot_general(
        twiddle, flat_rows, (((0,), (1,)), ((), ())), preferred_element_type=jnp.float32
    )
    fourier = fourier.reshape(order_total, 2, batch_size, chan_local, hemis, cycle_local)
    north = fourier[:, :, :, :, 0]
    south = fourier[:, :, :, :, 1]
    halves = jnp.stack([north + south, north - south], axis=4).astype(jnp.bfloat16)
    slot_count = legendre.shape[0]
    channel_groups = lax.axis_size("ch")
    first_slot = (lax.axis_index("ord") * channel_groups + lax.axis_index("ch")) * slot_count
    own_orders = lax.dynamic_slice_in_dim(order_table, first_slot, slot_count)
    transform = partial(legendre_sums, legendre=legendre, orders=own_orders)
    arrived = lax.all_to_all(
        lax.all_to_all(halves, "ord", split_axis=0, concat_axis=5, tiled=True),
        "ch",
        split_axis=0,
        concat_axis=3,
        tiled=True,
    )
    return transform(arrived)


def angle_tables(orders, length):
    factor = 1.0 / math.sqrt(length)
    step = 2.0 * math.pi / length
    column = jnp.arange(LANES, dtype=jnp.int32)
    fine = orders[:, None] * column[None, :] % length
    jumps = jnp.where(column == LANES - 1, length // 2, LANES * column)
    coarse = orders[:, None] * jumps[None, :] % length
    fine = fine.astype(jnp.float32) * step
    coarse = coarse.astype(jnp.float32) * step
    return jnp.stack([jnp.cos(fine) * factor, jnp.sin(fine) * factor, jnp.cos(coarse), jnp.sin(coarse)])


def exchange_kernel(
    sizes, orders, field, tables, affine, legendre, out,
    grid, rows, packed, twiddle, signs, sending, arrived, weights, wide, results, stats, stats_in, norms,
    field_sem, stats_out_sem, stats_in_sem, send_sem, recv_sem, own_sem, weight_sem, out_sem,
):
    n_ord, n_ch, cell_count = sizes
    total = n_ord * n_ch
    fields, hemis, cycles, length = grid.shape
    groups = twiddle.shape[0]
    steps = packed.shape[0]
    per_phase = legendre.shape[0] // groups
    tiles = rows.shape[1]
    own_ord, own_ch = lax.axis_index("ord"), lax.axis_index("ch")
    me = own_ord * n_ch + own_ch
    parts = field_sem.shape[0]
    per_part = fields // parts

    def load(part):
        span = pl.ds(part * per_part, per_part)
        return pltpu.make_async_copy(field.at[span], grid.at[span], field_sem.at[part])

    for part in range(parts):
        load(part).start()
    weight_load = pltpu.make_async_copy(legendre, weights, weight_sem)

    barrier = pltpu.get_barrier_semaphore()

    def greet(hop, carry):
        peer = lax.rem(me + hop, total)
        pl.semaphore_signal(
            barrier, inc=1, device_id=(peer // n_ch, lax.rem(peer, n_ch)), device_id_type=MESH
        )
        return carry

    lax.fori_loop(1, total, greet, 0)

    def fold(values):
        summed = values[:, :LANES]
        for tile in range(1, tiles - 1):
            summed += values[:, tile * LANES : (tile + 1) * LANES]
        rest = values[:, (tiles - 1) * LANES :]
        blank = jnp.zeros((1, LANES - rest.shape[1]), jnp.float32)
        return summed + jnp.concatenate([rest, blank], axis=1)

    for part in range(parts):
        load(part).wait()
        if part == parts - 1:
            weight_load.start()

        def measure(at, carry, part=part):
            row = part * per_part + at
            first = grid[row, 0].astype(jnp.float32)
            second = grid[row, 1].astype(jnp.float32)
            stats[pl.ds(row, 1), :] = fold(jnp.sum(first + second, axis=0, keepdims=True))
            stats[pl.ds(fields + row, 1), :] = fold(
                jnp.sum(first * first + second * second, axis=0, keepdims=True)
            )
            return carry

        lax.fori_loop(0, per_part, measure, 0)

    pl.semaphore_wait(barrier, total - 1)

    def stats_copy(hop):
        peer = lax.rem(own_ord + hop, n_ord)
        return pltpu.make_async_remote_copy(
            src_ref=stats,
            dst_ref=stats_in.at[own_ord],
            send_sem=stats_out_sem.at[hop],
            recv_sem=stats_in_sem.at[own_ord],
            device_id=(peer, own_ch),
            device_id_type=MESH,
        )

    for hop in range(1, n_ord):
        stats_copy(hop).start()
    stats_in[own_ord] = stats[...]

    def build(group, carry):
        span = pl.ds(pl.multiple_of(group * GROUP, GROUP), GROUP)
        cos_fine, sin_fine = tables[0, span, :], tables[1, span, :]
        cos_coarse, sin_coarse = tables[2, span, :], tables[3, span, :]
        sign = jnp.where(cos_coarse[:, LANES - 1 :] < 0.0, -1.0, 1.0)
        signs[group] = jnp.broadcast_to(sign, (GROUP, LANES))
        for tile in range(tiles):
            columns = slice(tile * LANES, (tile + 1) * LANES)
            cos_at, sin_at = cos_coarse[:, tile : tile + 1], sin_coarse[:, tile : tile + 1]
            twiddle[group, :GROUP, columns] = (cos_at * cos_fine - sin_at * sin_fine).astype(jnp.bfloat16)
            twiddle[group, GROUP:, columns] = (-(sin_at * cos_fine + cos_at * sin_fine)).astype(jnp.bfloat16)
        return carry

    lax.fori_loop(0, groups, build, 0)

    for hop in range(1, n_ord):
        peer = lax.rem(own_ord + hop, n_ord)
        pltpu.make_async_remote_copy(
            src_ref=stats, dst_ref=stats_in.at[peer], send_sem=stats_out_sem.at[hop],
            recv_sem=stats_in_sem.at[peer], device_id=(peer, own_ch), device_id_type=MESH,
        ).wait()

    merged = stats_in[0]
    for source in range(1, n_ord):
        merged = merged + stats_in[source]
    merged = jnp.sum(merged, axis=1, keepdims=True)
    average = merged[:fields] / cell_count
    spread = merged[fields:] / cell_count - average * average
    scale = lax.rsqrt(spread + 1e-05) * affine[0, :, :1]
    norms[0] = jnp.broadcast_to(average, (fields, LANES))
    norms[1] = jnp.broadcast_to(scale, (fields, LANES))
    norms[2] = affine[1]

    def normalize(at, carry, begin, count):
        shift = norms[0, pl.ds(at, 1), :]
        factor = norms[1, pl.ds(at, 1), :]
        offset = norms[2, pl.ds(at, 1), :]
        for hemi in range(hemis):
            for tile in range(tiles):
                piece = grid[at, hemi, begin : begin + count, tile * LANES : min((tile + 1) * LANES, length)]
                across = piece.shape[1]
                piece = (piece.astype(jnp.float32) - shift[:, :across]) * factor[:, :across] + offset[:, :across]
                if across < LANES:
                    piece = jnp.concatenate([piece, jnp.zeros((count, LANES - across), jnp.float32)], axis=1)
                rows[hemi, tile, pl.ds(at, count, stride=PITCH), :] = piece
        return carry

    lane = lax.broadcasted_iota(jnp.int32, (GROUP, LANES), 1)
    low = lane // fields % 2 == 0
    high = lane // (2 * fields) % 2 == 0

    def swap(mask, upper, lower, amount):
        return (
            jnp.where(mask, upper, pltpu.roll(lower, amount, 1)),
            jnp.where(mask, pltpu.roll(upper, LANES - amount, 1), lower),
        )

    sub = lax.broadcasted_iota(jnp.int32, (GROUP // 8, 8, LANES), 1)
    top = sub < per_phase

    def weave(first, second):
        first, second = first.reshape(GROUP // 8, 8, LANES), second.reshape(GROUP // 8, 8, LANES)
        return (
            jnp.where(top, first, pltpu.roll(second, per_phase, 1)),
            jnp.where(top, pltpu.roll(first, per_phase, 1), second),
        )

    def transform(phase, step):
        spectrum = lax.dot_general(
            twiddle[phase], packed[step], (((1,), (1,)), ((), ())), preferred_element_type=jnp.float32
        )
        sign = signs[phase]
        sign = jnp.concatenate([sign, sign], axis=0)
        north, south = spectrum[:, :LANES], spectrum[:, LANES:] * sign
        even, odd = north + south, north - south
        a, b, c, d = even[:GROUP], even[GROUP:], odd[:GROUP], odd[GROUP:]
        a, b = swap(low, a, b, fields)
        c, d = swap(low, c, d, fields)
        a, c = swap(high, a, c, 2 * fields)
        b, d = swap(high, b, d, 2 * fields)
        front, back = weave(a, b), weave(c, d)
        for side in range(2):
            both = jnp.concatenate([front[side], back[side]], axis=1)
            sending[phase, :, side, step] = both.astype(jnp.bfloat16)

        def send(hop, inner):
            ring = lax.rem(own_ch + hop // n_ord + n_ch // 2, n_ch)
            side = lax.rem(own_ord + hop, n_ord)
            peer = side * n_ch + ring
            pltpu.make_async_remote_copy(
                src_ref=sending.at[phase, peer // 2, lax.rem(peer, 2), step],
                dst_ref=arrived.at[phase, own_ch, own_ord, step],
                send_sem=send_sem.at[phase, peer],
                recv_sem=recv_sem.at[phase, me],
                device_id=(side, ring),
                device_id_type=MESH,
            ).start()
            return inner

        lone = n_ch // 2 * n_ord
        lax.fori_loop(0, lone, send, 0)
        lax.fori_loop(lone + 1, total, send, 0)

    for begin in range(0, cycles, 16):
        count = min(16, cycles - begin)

        lax.fori_loop(0, fields, partial(normalize, begin=begin, count=count), 0)

        def prepare(at, carry, begin=begin):
            step = begin // QUAD + at
            for hemi in range(hemis):
                for quarter in range(QUAD):
                    span = pl.ds(pl.multiple_of((at * QUAD + quarter) * PITCH, 8), fields)
                    place = hemi * LANES + quarter * fields
                    for tile in range(tiles):
                        packed[step, place : place + fields, tile * LANES : (tile + 1) * LANES] = rows[
                            hemi, tile, span, :
                        ].astype(jnp.bfloat16)
            transform(0, step)
            return carry

        lax.fori_loop(0, count // QUAD, prepare, 0)

    def rest(at, carry):
        transform(1 + at // steps, lax.rem(at, steps))
        return carry

    lax.fori_loop(0, (groups - 1) * steps, rest, 0)

    def own_copy(phase):
        return pltpu.make_async_copy(
            sending.at[phase, me // 2, lax.rem(me, 2)], arrived.at[phase, own_ch, own_ord], own_sem.at[phase]
        )

    def out_copy(phase):
        return pltpu.make_async_copy(
            results.at[lax.rem(phase, 2)], out.at[pl.ds(phase * per_phase, per_phase)], out_sem.at[phase]
        )

    for phase in range(groups):
        own_copy(phase).start()
    weight_load.wait()
    batch, local = results.shape[4], results.shape[5] // n_ch
    half = LANES // 2
    depth = n_ord * cycles

    def conclude(phase, carry):
        def finish(hop, inner):
            peer = lax.rem(me + hop, total)
            pltpu.make_async_remote_copy(
                src_ref=sending.at[phase, peer // 2, lax.rem(peer, 2)],
                dst_ref=arrived.at[phase, lax.rem(peer, n_ch), peer // n_ch],
                send_sem=send_sem.at[phase, peer],
                recv_sem=recv_sem.at[phase, peer],
                device_id=(peer // n_ch, lax.rem(peer, n_ch)),
                device_id_type=MESH,
            ).wait()
            return inner

        lax.fori_loop(1, total, finish, 0)
        own_copy(phase).wait()

        @pl.when(phase >= 2)
        def _():
            out_copy(phase - 2).wait()

        for source in range(n_ch):
            wide[source] = arrived[phase, source].astype(jnp.float32).reshape(depth * per_phase, LANES)

        def analyze(at, inner):
            slot = phase * per_phase + at
            order = orders[me * legendre.shape[0] + slot]
            turned = [
                wide[source, pl.ds(at, depth, stride=per_phase), :].T.astype(jnp.bfloat16)
                for source in range(n_ch)
            ]
            for parity in range(2):
                left = jnp.concatenate([t[parity * half : (parity + 1) * half] for t in turned], axis=0)
                sums = jnp.dot(left, weights[slot, parity], preferred_element_type=jnp.float32)
                degree = 2 * lax.broadcasted_iota(jnp.int32, sums.shape, 1) + parity
                sums = jnp.where(degree >= order, sums, 0.0).astype(jnp.bfloat16)
                for source in range(n_ch):
                    results[lax.rem(phase, 2), at, parity, :, :, source * local : (source + 1) * local, :] = sums[
                        source * half : (source + 1) * half
                    ].reshape(2, batch, local, sums.shape[1])
            return inner

        lax.fori_loop(0, per_phase, analyze, 0)
        out_copy(phase).start()
        return carry

    lax.fori_loop(0, groups, conclude, 0)
    for phase in range(groups - 2, groups):
        out_copy(phase).wait()


def kernel_path(field_grid, norm_gain, norm_bias, order_table, legendre):
    batch, local, hemis, cycles, length = field_grid.shape
    n_ord, n_ch = lax.axis_size("ord"), lax.axis_size("ch")
    order_total, slots = order_table.shape[0], legendre.shape[0]
    fields = batch * local
    groups = order_total // GROUP
    tiles = -(-length // LANES)
    steps = cycles // QUAD
    total = n_ord * n_ch
    per_phase = slots // groups
    half_degrees = legendre.shape[3]
    phased = order_table.reshape(total, groups, per_phase).swapaxes(0, 1).reshape(order_total)
    tables = angle_tables(phased, length)
    affine = jnp.stack([norm_gain, norm_bias])[:, None, :, None]
    affine = jnp.broadcast_to(affine, (2, batch, local, LANES)).reshape(2, fields, LANES)
    vmem = pl.BlockSpec(memory_space=pltpu.VMEM)
    hbm = pl.BlockSpec(memory_space=pltpu.HBM)
    depth = n_ord * cycles
    result = (2, 2, batch, n_ch * local, half_degrees)
    return pl.pallas_call(
        partial(exchange_kernel, (n_ord, n_ch, hemis * cycles * n_ord * length)),
        out_shape=jax.ShapeDtypeStruct((slots,) + result, jnp.bfloat16),
        in_specs=[pl.BlockSpec(memory_space=pltpu.SMEM), hbm, vmem, vmem, hbm],
        out_specs=hbm,
        scratch_shapes=[
            pltpu.VMEM((fields, hemis, cycles, length), jnp.bfloat16),
            pltpu.VMEM((hemis, tiles, 16 * PITCH, LANES), jnp.float32),
            pltpu.VMEM((steps, hemis * LANES, tiles * LANES), jnp.bfloat16),
            pltpu.VMEM((groups, 2 * GROUP, tiles * LANES), jnp.bfloat16),
            pltpu.VMEM((groups, GROUP, LANES), jnp.float32),
            pltpu.VMEM((groups, total // 2, 2, steps, QUAD * per_phase, LANES), jnp.bfloat16),
            pltpu.VMEM((groups, n_ch, n_ord, steps, QUAD * per_phase, LANES), jnp.bfloat16),
            pltpu.VMEM(legendre.shape, jnp.bfloat16),
            pltpu.VMEM((n_ch, depth * per_phase, LANES), jnp.float32),
            pltpu.VMEM((2, per_phase) + result, jnp.bfloat16),
            pltpu.VMEM((2 * fields, LANES), jnp.float32),
            pltpu.VMEM((n_ord, 2 * fields, LANES), jnp.float32),
            pltpu.VMEM((3, fields, LANES), jnp.float32),
            pltpu.SemaphoreType.DMA((8,)),
            pltpu.SemaphoreType.DMA((n_ord,)),
            pltpu.SemaphoreType.DMA((n_ord,)),
            pltpu.SemaphoreType.DMA((groups, total)),
            pltpu.SemaphoreType.DMA((groups, total)),
            pltpu.SemaphoreType.DMA((groups,)),
            pltpu.SemaphoreType.DMA,
            pltpu.SemaphoreType.DMA((groups,)),
        ],
        compiler_params=pltpu.CompilerParams(
            collective_id=0, has_side_effects=True, vmem_limit_bytes=63 * 2**20
        ),
        name="spectral_analysis",
    )(order_table, field_grid.reshape(fields, hemis, cycles, length), tables, affine, legendre)


def on_device(field_grid, norm_gain, norm_bias, order_table, legendre):
    batch, local, hemis, cycles, _ = field_grid.shape
    fits = (
        batch * local * QUAD == LANES
        and hemis == 2
        and cycles % QUAD == 0
        and legendre.shape[0] == 16
        and order_table.shape[0] == 4 * GROUP
        and field_grid.shape[4] <= LANES * (LANES - 1)
        and field_grid.shape[4] % 2 == 0
    )
    path = kernel_path if fits else general_path
    return path(field_grid, norm_gain, norm_bias, order_table, legendre)


def solution(mesh):
    placed = (
        P(None, "ch", None, "ord", None),
        P("ch"),
        P("ch"),
        P(),
        P(("ord", "ch"), None, None, None),
    )
    return jax.shard_map(
        on_device,
        mesh=mesh,
        in_specs=placed,
        out_specs=P(("ord", "ch"), None, None, None, None, None),
        check_vma=False,
    )
```

time: 200 us -> 172 us (0.86)
  Pallas kernels: 183 us -> 150 us
  local copies, waits for them, and re-layouts: 12.5 us -> 17.7 us
    pallas_call x1 -> x0, Pallas kernels: 20.1 us -> none  [kernel_path(): pl.pallas_call(legendre_kernel, grid=(slots,), out_shape=jax.ShapeDtypeSt...]
    pallas_call x1, Pallas kernels: 163 us -> 150 us  [kernel_path(): pl.pallas_call(partial(exchange_kernel, (n_ord, n_ch, hemis * cycles * n_...]
    unnamed x9 -> x2, local copies, waits for them, and re-layouts: 9.31 us -> 16 us
    cos x1 -> x0, other arithmetic: 2.92 us -> none  [angle_tables(): jnp.cos(coarse)]
    mul x1, other arithmetic: 0.01 us -> 2.25 us  [angle_tables(): jnp.cos(fine) * factor]
where the time goes in v2:
time: 172 us; the launch traced here: 171 us
  Pallas kernels  150 us (87%)
  local copies, waits for them, and re-layouts  17.7 us (10%)
  other arithmetic  3.97 us (2%)
    pallas_call x1, Pallas kernels, kernel_path(): pl.pallas_call(partial(exchange_kernel, (n_ord, n_ch, hemis * cycles * n_...  150 us
    unnamed x2, local copies, waits for them, and re-layouts  16 us

profile of v2, /device:TPU:0, one launch (start us, length us, event | category | flops | bytes accessed | tf_op | source)
XLA Modules:
  0.0 171.4 jit_solution(14867677177244431382)
XLA Ops:
  0.0 0.7 pad_maximum_fusion.1
  0.7 0.1 broadcast_in_dim.18
  0.8 0.7 broadcast_in_dim.19.affine
  1.5 0.8 reshape.255
  2.3 0.1 mul.106
  2.4 2.2 %cosine_multiply_fusion = (f32[1,512,128]{2,1,0:T(8,128)S(1)}, f32[1,512,128]{2,1,0:T(8,128)S(1)}, f32[1,512,128]{2,1,0:T(8,128)S(1)}, f32[1,512,128]{2,1,0:T(8,128)S(1)}) fusion(s32[512]{0:T(512)S(1)} %mul.106, s32[128]{0:T(128)S(1)} %compare_select_fusion), kind=kLoop, calls=%fused_computation.13 | loop fusion | flops 1310720 | bytes 1051136 | tf_op jit(solution)/shard_map/mul | solution.py:91
  4.7 1.0 pad_maximum_fusion.tables
  5.7 9.2 %copy.7 = bf16[2,16,2,44,1440]{4,3,2,1,0:T(8,128)(2,1)} copy(bf16[2,16,2,44,1440]{4,2,3,1,0:T(2,128)(2,1)} %param.5) | data formatting | bytes 16220160 | tf_op args[0]
  14.9 149.7 %spectral_analysis.1 = bf16[16,2,2,2,64,360]{5,4,3,2,1,0:T(8,128)(2,1)} custom-call(s32[512]{0:T(512)} %orders.1, bf16[32,2,44,1440]{3,2,1,0:T(8,128)(2,1)} %bitcast.4, f32[4,512,128]{2,1,0:T(8,128)} %pad_maximum_fusion.tables, f32[2,32,128]{2,1,0:T(8,128)} %broadcast_in_dim.19.affine, bf16[16,2,352,360]{3,2,1,0:T(8,128)(2,1)} %legendre.1), custom_call_target="tpu_custom_call" | custom-call | tf_op jit(solution)/shard_map/spectral_analysis/pallas_call | solution.py:387
  164.7 6.8 %copy.10 = bf16[16,2,2,2,64,360]{5,4,3,2,1,0:T(8,128)(2,1)} copy(bf16[16,2,2,2,64,360]{5,4,3,2,1,0:T(8,128)(2,1)} %spectral_analysis.1) | data formatting | bytes 11796480
  (3 shorter events, 0.0 us)

commit v3 on v2

--- a/solution.py
+++ b/solution.py
@@ -88,11 +88,11 @@
     coarse = orders[:, None] * jumps[None, :] % length
     fine = fine.astype(jnp.float32) * step
     coarse = coarse.astype(jnp.float32) * step
-    return jnp.stack([jnp.cos(fine) * factor, jnp.sin(fine) * factor, jnp.cos(coarse), jnp.sin(coarse)])
+    return jnp.cos(fine) * factor, jnp.sin(fine) * factor, jnp.cos(coarse), jnp.sin(coarse)
 
 
 def exchange_kernel(
-    sizes, orders, field, tables, affine, legendre, out,
+    sizes, orders, field, cos_fines, sin_fines, cos_coarses, sin_coarses, affine, legendre, out,
     grid, rows, packed, twiddle, signs, sending, arrived, weights, wide, results, stats, stats_in, norms,
     field_sem, stats_out_sem, stats_in_sem, send_sem, recv_sem, own_sem, weight_sem, out_sem,
 ):
@@ -171,8 +171,8 @@
 
     def build(group, carry):
         span = pl.ds(pl.multiple_of(group * GROUP, GROUP), GROUP)
-        cos_fine, sin_fine = tables[0, span, :], tables[1, span, :]
-        cos_coarse, sin_coarse = tables[2, span, :], tables[3, span, :]
+        cos_fine, sin_fine = cos_fines[span, :], sin_fines[span, :]
+        cos_coarse, sin_coarse = cos_coarses[span, :], sin_coarses[span, :]
         sign = jnp.where(cos_coarse[:, LANES - 1 :] < 0.0, -1.0, 1.0)
         signs[group] = jnp.broadcast_to(sign, (GROUP, LANES))
         for tile in range(tiles):
@@ -182,7 +182,7 @@
             twiddle[group, GROUP:, columns] = (-(sin_at * cos_fine + cos_at * sin_fine)).astype(jnp.bfloat16)
         return carry
 
-    lax.fori_loop(0, groups, build, 0)
+    build(0, 0)
 
     for hop in range(1, n_ord):
         peer = lax.rem(own_ord + hop, n_ord)
@@ -272,8 +272,10 @@
         lax.fori_loop(0, lone, send, 0)
         lax.fori_loop(lone + 1, total, send, 0)
 
-    for begin in range(0, cycles, 16):
-        count = min(16, cycles - begin)
+    begin = count = 0
+    while begin + count < cycles:
+        begin += count
+        count = min(16 if begin else 8, cycles - begin)
 
         lax.fori_loop(0, fields, partial(normalize, begin=begin, count=count), 0)
 
@@ -291,6 +293,8 @@
             return carry
 
         lax.fori_loop(0, count // QUAD, prepare, 0)
+
+    lax.fori_loop(1, groups, build, 0)
 
     def rest(at, carry):
         transform(1 + at // steps, lax.rem(at, steps))
@@ -387,7 +391,7 @@
     return pl.pallas_call(
         partial(exchange_kernel, (n_ord, n_ch, hemis * cycles * n_ord * length)),
         out_shape=jax.ShapeDtypeStruct((slots,) + result, jnp.bfloat16),
-        in_specs=[pl.BlockSpec(memory_space=pltpu.SMEM), hbm, vmem, vmem, hbm],
+        in_specs=[pl.BlockSpec(memory_space=pltpu.SMEM), hbm, vmem, vmem, vmem, vmem, vmem, hbm],
         out_specs=hbm,
         scratch_shapes=[
             pltpu.VMEM((fields, hemis, cycles, length), jnp.bfloat16),
@@ -416,7 +420,7 @@
             collective_id=0, has_side_effects=True, vmem_limit_bytes=63 * 2**20
         ),
         name="spectral_analysis",
-    )(order_table, field_grid.reshape(fields, hemis, cycles, length), tables, affine, legendre)
+    )(order_table, field_grid.reshape(fields, hemis, cycles, length), *tables, affine, legendre)
 
 
 def on_device(field_grid, norm_gain, norm_bias, order_table, legendre):

time: 172 us -> 171 us (level)
    sin x0 -> x1, other arithmetic: none -> 3.29 us  [angle_tables(): jnp.sin(coarse)]
    mul x1 -> x0, other arithmetic: 2.25 us -> none  [angle_tables(): jnp.cos(fine) * factor]
where the time goes in v3:
time: 171 us
  Pallas kernels  149 us (87%)
  local copies, waits for them, and re-layouts  17.7 us (10%)
  other arithmetic  3.98 us (2%)
    pallas_call x1, Pallas kernels, kernel_path(): pl.pallas_call(partial(exchange_kernel, (n_ord, n_ch, hemis * cycles * n_...  149 us
    unnamed x2, local copies, waits for them, and re-layouts  16 us

profile of v3, /device:TPU:0, one launch (start us, length us, event | category | flops | bytes accessed | tf_op | source)
XLA Modules:
  0.0 170.5 jit_solution(18293382960946127334)
XLA Ops:
  0.0 0.7 pad_maximum_fusion
  0.7 0.1 broadcast_in_dim.18
  0.8 0.7 broadcast_in_dim.19.affine
  1.5 0.8 reshape.18
  2.3 0.1 mul.48
  2.4 3.3 %fusion.6 = (f32[512,128]{1,0:T(8,128)}, f32[512,128]{1,0:T(8,128)}, f32[512,128]{1,0:T(8,128)}, f32[512,128]{1,0:T(8,128)}) fusion(s32[128]{0:T(128)S(1)} %compare_select_fusion, s32[512]{0:T(512)S(1)} %mul.48), kind=kLoop, calls=%fused_computation.9 | loop fusion | flops 1310720 | bytes 1051136 | tf_op jit(solution)/shard_map/sin | solution.py:91
  5.7 9.2 %copy.7 = bf16[2,16,2,44,1440]{4,3,2,1,0:T(8,128)(2,1)} copy(bf16[2,16,2,44,1440]{4,2,3,1,0:T(2,128)(2,1)} %param.5) | data formatting | bytes 16220160 | tf_op args[0]
  14.9 148.8 %spectral_analysis.1 = bf16[16,2,2,2,64,360]{5,4,3,2,1,0:T(8,128)(2,1)} custom-call(s32[512]{0:T(512)} %orders.1, bf16[32,2,44,1440]{3,2,1,0:T(8,128)(2,1)} %bitcast.4, f32[512,128]{1,0:T(8,128)} %get-tuple-element.8.cos_fines, f32[512,128]{1,0:T(8,128)} %get-tuple-element.7.sin_fines, f32[512,128]{1,0:T(8,128)} %get-tuple-element.6.cos_coarses, ...), custom_call_target="tpu_custom_call" | custom-call | tf_op jit(solution)/shard_map/spectral_analysis/pallas_call | solution.py:391
  163.8 6.8 %copy.10 = bf16[16,2,2,2,64,360]{5,4,3,2,1,0:T(8,128)(2,1)} copy(bf16[16,2,2,2,64,360]{5,4,3,2,1,0:T(8,128)(2,1)} %spectral_analysis.1) | data formatting | bytes 11796480
  (3 shorter events, 0.0 us)

commit v4 on v3

--- a/solution.py
+++ b/solution.py
@@ -367,6 +367,24 @@
     lax.fori_loop(0, groups, conclude, 0)
     for phase in range(groups - 2, groups):
         out_copy(phase).wait()
+
+
+def emit_kernel(source, target, held, in_sem, out_sem):
+    count = held.shape[0]
+
+    def load(at):
+        return pltpu.make_async_copy(source.at[at], held.at[at], in_sem.at[at])
+
+    def store(at):
+        return pltpu.make_async_copy(held.at[at], target.at[at], out_sem.at[at])
+
+    for at in range(count):
+        load(at).start()
+    for at in range(count):
+        load(at).wait()
+        store(at).start()
+    for at in range(count):
+        store(at).wait()
 
 
 def kernel_path(field_grid, norm_gain, norm_bias, order_table, legendre):
@@ -388,7 +406,7 @@
     hbm = pl.BlockSpec(memory_space=pltpu.HBM)
     depth = n_ord * cycles
     result = (2, 2, batch, n_ch * local, half_degrees)
-    return pl.pallas_call(
+    summed = pl.pallas_call(
         partial(exchange_kernel, (n_ord, n_ch, hemis * cycles * n_ord * length)),
         out_shape=jax.ShapeDtypeStruct((slots,) + result, jnp.bfloat16),
         in_specs=[pl.BlockSpec(memory_space=pltpu.SMEM), hbm, vmem, vmem, vmem, vmem, vmem, hbm],
@@ -421,6 +439,18 @@
         ),
         name="spectral_analysis",
     )(order_table, field_grid.reshape(fields, hemis, cycles, length), *tables, affine, legendre)
+    return pl.pallas_call(
+        emit_kernel,
+        out_shape=jax.ShapeDtypeStruct(summed.shape, summed.dtype),
+        in_specs=[hbm],
+        out_specs=hbm,
+        scratch_shapes=[
+            pltpu.VMEM(summed.shape, summed.dtype),
+            pltpu.SemaphoreType.DMA((slots,)),
+            pltpu.SemaphoreType.DMA((slots,)),
+        ],
+        name="emit_result",
+    )(summed)
 
 
 def on_device(field_grid, norm_gain, norm_bias, order_table, legendre):

time: 171 us -> 169 us (0.988)
  local copies, waits for them, and re-layouts: 17.7 us -> 10.9 us
  Pallas kernels: 149 us -> 154 us
    unnamed x2 -> x1, local copies, waits for them, and re-layouts: 16 us -> 9.25 us
    pallas_call x0 -> x1, Pallas kernels: none -> 5.48 us  [kernel_path(): pl.pallas_call(emit_kernel, out_shape=jax.ShapeDtypeStruct(summed.shape,...]
where the time goes in v4:
time: 169 us
  Pallas kernels  154 us (91%)
  local copies, waits for them, and re-layouts  10.9 us (6%)
  other arithmetic  3.98 us (2%)
    pallas_call x1, Pallas kernels, kernel_path(): pl.pallas_call(partial(exchange_kernel, (n_ord, n_ch, hemis * cycles * n_...  149 us
    unnamed x1, local copies, waits for them, and re-layouts  9.25 us
    pallas_call x1, Pallas kernels, kernel_path(): pl.pallas_call(emit_kernel, out_shape=jax.ShapeDtypeStruct(summed.shape,...  5.48 us

profile of v4, /device:TPU:0, one launch (start us, length us, event | category | flops | bytes accessed | tf_op | source)
XLA Modules:
  0.0 169.3 jit_solution(15172771122882594191)
XLA Ops:
  0.0 0.7 pad_maximum_fusion
  0.7 0.1 broadcast_in_dim.18
  0.8 0.7 broadcast_in_dim.19.affine
  1.5 0.8 reshape.18
  2.3 0.1 mul.48
  2.4 3.3 %fusion.6 = (f32[512,128]{1,0:T(8,128)}, f32[512,128]{1,0:T(8,128)}, f32[512,128]{1,0:T(8,128)}, f32[512,128]{1,0:T(8,128)}) fusion(s32[128]{0:T(128)S(1)} %compare_select_fusion, s32[512]{0:T(512)S(1)} %mul.48), kind=kLoop, calls=%fused_computation.9 | loop fusion | flops 1310720 | bytes 1051136 | tf_op jit(solution)/shard_map/sin | solution.py:91
  5.7 9.2 %copy.7 = bf16[2,16,2,44,1440]{4,3,2,1,0:T(8,128)(2,1)} copy(bf16[2,16,2,44,1440]{4,2,3,1,0:T(2,128)(2,1)} %param.5) | data formatting | bytes 16220160 | tf_op args[0]
  14.9 148.8 %spectral_analysis.1.source = bf16[16,2,2,2,64,360]{5,4,3,2,1,0:T(8,128)(2,1)} custom-call(s32[512]{0:T(512)} %orders.1, bf16[32,2,44,1440]{3,2,1,0:T(8,128)(2,1)} %bitcast.4, f32[512,128]{1,0:T(8,128)} %get-tuple-element.8.cos_fines, f32[512,128]{1,0:T(8,128)} %get-tuple-element.7.sin_fines, f32[512,128]{1,0:T(8,128)} %get-tuple-element.6.cos_coarses, ...), custom_call_target="tpu_custom_call" | custom-call | tf_op jit(solution)/shard_map/spectral_analysis/pallas_call | solution.py:409
  163.8 5.5 %emit_result.1 = bf16[16,2,2,2,64,360]{5,4,3,2,1,0:T(8,128)(2,1)} custom-call(bf16[16,2,2,2,64,360]{5,4,3,2,1,0:T(8,128)(2,1)} %spectral_analysis.1.source), custom_call_target="tpu_custom_call" | custom-call | tf_op jit(solution)/shard_map/emit_result/pallas_call | solution.py:442
  (3 shorter events, 0.0 us)
